TPU v7x, 256 devices: a whole 4x4x8 slice. The times are simulated.
256 devices in a mesh: depth: 64 (over x, z, core), strip: 4 (over y).
Axes of the slice: x: 4, y: 4, z: 8, core: 2. Of those that a mesh axis runs over, the one named last changes fastest.
Arguments:
- density: bfloat16 [256, 64, 1024], P('depth', 'strip'), may hold values from -6 to 6
- tf_bins: int32 [256, 64, 1024], P('depth', 'strip'), may hold values from 0 to 15
- tf_table: float32 [4, 16], replicated, may hold values from 0.2 to 2
- brick_order: int32 [4, 64], P('strip'), may hold values from 0 to 63, each once within a row
Outputs:
- image: float32 [4, 65536], P(None, ('strip', 'depth'))
Inputs may be any that keep to these rules, and one draw needn't show every extreme that they name: `tf_bins`: each voxel's bin indexes a column of tf_table. `brick_order`: each row lists every brick once.
All inputs are finite; a program needn't handle non-finite values.
Results may differ from a plain program's by a relative error of at most 0.0017.
Values may be sent and summed in bfloat16 or wider, within the bound.
A program may use at most 64 MiB of HBM per device.

v0:
```python
import jax
import jax.numpy as jnp
from jax import lax
from jax.sharding import PartitionSpec as P

LIGHT_X = 0.36
LIGHT_Y = 0.48
LIGHT_Z = 0.8
SHADE_GAIN = 1.5


def with_halo(cells, sides, width):
    for axis, dim in sides:
        count = lax.axis_size(axis)
        ends = count - 1
        head = lax.slice_in_dim(cells, 0, width, axis=dim)
        tail = lax.slice_in_dim(cells, cells.shape[dim] - width, cells.shape[dim], axis=dim)
        cells = jnp.concatenate(
            [
                lax.ppermute(tail, axis, [(i, (i + 1) % count) for i in range(ends)]),
                cells,
                lax.ppermute(head, axis, [((i + 1) % count, i) for i in range(ends)]),
            ],
            axis=dim,
        )
    return cells


def shear_plane(values, plane_index):
    across = values.shape[-1]
    offset = 3 * plane_index // 8
    fraction = (3 * plane_index % 8).astype(jnp.float32) / 8.0
    columns = jnp.arange(across, dtype=jnp.int32)
    first = jnp.where(columns < across - offset, jnp.roll(values, -offset, axis=2), 0.0)
    second = jnp.where(columns < across - offset - 1, jnp.roll(first, -1, axis=2), 0.0)
    return (1.0 - fraction) * first + fraction * second


def plane_terms(window, tf_plane, tf_table, plane_index, total_planes):
    beneath = window[0]
    middle = window[1]
    overhead = window[2]
    centre = middle[1:-1]
    sideways = jnp.pad(centre, ((0, 0), (1, 1)))
    slope_across = 0.5 * (sideways[:, 2:] - sideways[:, :-2])
    slope_down = 0.5 * (middle[2:] - middle[:-2])
    slope_deep = 0.5 * (overhead[1:-1] - beneath[1:-1])
    lengths = jnp.sqrt(
        1.0 + slope_across * slope_across + slope_down * slope_down + slope_deep * slope_deep
    )
    shading = (LIGHT_X * slope_across + LIGHT_Y * slope_down + LIGHT_Z * slope_deep) / lengths
    classes = jnp.arange(tf_table.shape[1], dtype=jnp.int32)
    onehot = (tf_plane[None, :, :] == classes[:, None, None]).astype(jnp.float32)
    looked = jnp.einsum("cm,myx->cyx", tf_table, onehot, precision=lax.Precision.HIGHEST)
    extinction = looked[0] * (1.0 + centre * centre) / total_planes
    opacity = 1.0 - jnp.exp(-extinction)
    emitted = looked[1:] * (opacity * jnp.exp(SHADE_GAIN * shading))[None]
    return shear_plane(jnp.concatenate([extinction[None], emitted], axis=0), plane_index)


def order_mask(sequence):
    bricks = sequence.shape[0]
    slots = jnp.arange(bricks, dtype=jnp.int32)
    onehot = (sequence[:, None] == slots[None, :]).astype(jnp.int32)
    position = jnp.sum(onehot * slots[:, None], axis=0)
    return (position[None, :] < position[:, None]).astype(jnp.float32)


def per_device(density, tf_bins, tf_table, brick_order):
    planes = density.shape[0]
    height = density.shape[1]
    across = density.shape[2]
    bricks = lax.axis_size("depth")
    block = with_halo(density, (("depth", 0), ("strip", 1)), 1)
    first_plane = lax.axis_index("depth") * planes
    total_planes = planes * bricks
    colour = jnp.zeros((3, height, across), jnp.float32)
    depth_sum = jnp.zeros((height, across), jnp.float32)
    for plane_at in range(planes):
        window = block[plane_at : plane_at + 3].astype(jnp.float32)
        sheared = plane_terms(
            window, tf_bins[plane_at], tf_table, first_plane + plane_at, total_planes
        )
        colour = colour + jnp.exp(-depth_sum)[None] * sheared[1:]
        depth_sum = depth_sum + sheared[0]
    pixels = height * across
    before = order_mask(brick_order[0])
    flat_colour = colour.reshape(3, pixels)
    flat_depth = depth_sum.reshape(1, pixels)
    partial_value = jnp.concatenate([flat_colour, flat_depth], axis=0)[:, None, :]
    received = lax.all_to_all(
        partial_value.astype(jnp.bfloat16), "depth", split_axis=2, concat_axis=1, tiled=True
    ).astype(partial_value.dtype)
    depths = received[3]
    prefix = jnp.dot(before, depths, precision=lax.Precision.HIGHEST)
    weight = jnp.exp(-prefix)
    shown = jnp.sum(weight[None] * received[:3], axis=1)
    remaining = jnp.exp(-jnp.sum(depths, axis=0))
    return jnp.concatenate([shown, remaining[None]], axis=0)


def solution(mesh):
    in_specs = (P("depth", "strip", None), P("depth", "strip", None), P(), P("strip", None))
    out_specs = P(None, ("strip", "depth"))
    return jax.shard_map(
        per_device, mesh=mesh, in_specs=in_specs, out_specs=out_specs, check_vma=False
    )
```

profile of v0, /device:TPU:1, one launch (start us, length us, event | category | flops | bytes accessed | tf_op | source)
XLA Modules:
  0.0 676.8 jit_solution(5689342530783288285)
XLA Ops:
  0.0 0.0 copy-start
  0.0 0.8 fusion.84
  0.8 4.9 collective-permute-start
  5.7 1.9 collective-permute-start.1
  7.7 1.0 slice_bitcast_fusion.1
  8.7 0.0 copy-done
  8.7 0.4 fusion.1
  9.1 0.4 convolution_bitcast_fusion.1
  9.6 0.4 fusion.2
  10.0 0.4 convolution_bitcast_fusion
  10.5 0.0 collective-permute-done
  10.5 0.9 constant_dynamic-update-slice_fusion.1
  11.4 0.0 collective-permute-done.1
  11.5 3.2 collective-permute-start.2
  14.7 1.3 collective-permute-start.3
  16.1 0.2 copy.133
  16.3 0.2 copy.132
  16.6 0.0 collective-permute-done.2
  16.6 2.6 collective-permute-done.3
  19.2 0.1 pad_maximum_fusion
  19.4 0.1 slice_convert_fusion.1
  19.6 0.2 fusion.61
  19.8 0.1 slice_multiply_fusion.3
  19.9 0.1 copy.84
  19.9 0.7 fusion.21
  20.6 0.2 slice.353
  20.9 0.2 fusion.17
  21.1 0.1 slice.365
  21.3 0.2 fusion.43
  21.5 0.1 slice_multiply_fusion.1
  21.6 0.1 copy.96
  21.7 0.7 fusion.9
  22.3 0.2 slice.389
  22.6 0.2 broadcast_multiply_fusion
  22.8 0.1 slice.377
  22.9 0.2 fusion.29
  23.2 0.7 fusion.27
  23.8 0.1 slice.355
  23.9 0.2 negate_exponential_fusion.1
  24.2 0.1 pad_maximum_fusion.1
  24.2 0.3 copy_add_fusion
  24.6 0.7 fusion.31
  25.2 0.2 negate_exponential_fusion
  25.4 0.1 fusion.33
  25.6 0.3 fusion.24
  25.9 0.1 pad_maximum_fusion.2
  26.0 13.2 %copy.98 = bf16[4,1,16384]{0,1,2:T(2,128)(2,1)} copy(bf16[4,1,16384]{2,0,1:T(4,128)(2,1)S(1)} %pad_maximum_fusion.2) | data formatting | bytes 262144 | tf_op jit(solution)/shard_map/concatenate | solution.py:90
  39.2 0.5 broadcast.130
  39.7 0.0 copy-start.2
  39.7 90.8 %reduce.6 = bf16[16384,4]{1,0:T(8,128)(2,1)} reduce(bf16[16384,1,4]{2,1,0:T(2,128)(2,1)} %bitcast.201, bf16[]{:T(256)} %broadcast.130), dimensions={1}, to_apply=%bitcast.190.reduce_sub_computation | reduce | bytes 262146
  130.4 9.3 %reshape.196 = bf16[64,2,512]{2,1,0:T(2,128)(2,1)} reshape(bf16[16384,4]{1,0:T(8,128)(2,1)} %reduce.6) | data formatting | bytes 262144
  139.8 14.3 %all-to-all-start = ((bf16[64,2,512]{2,1,0:T(2,128)(2,1)}), bf16[64,2,512]{2,1,0:T(2,128)(2,1)S(1)}, u32[]{:S(2)}, u32[]{:S(2)}) async-start(bf16[64,2,512]{2,1,0:T(2,128)(2,1)} %reshape.196), calls=%async_computation | async-start | bytes 262144 | tf_op jit(solution)/shard_map/all_to_all | solution.py:91
  154.1 0.0 copy-done.2
  154.1 0.1 select_reduce_fusion
  154.2 10.2 %all-to-all-done = bf16[64,2,512]{2,1,0:T(2,128)(2,1)S(1)} async-done(((bf16[64,2,512]{2,1,0:T(2,128)(2,1)}), bf16[64,2,512]{2,1,0:T(2,128)(2,1)S(1)}, u32[]{:S(2)}, u32[]{:S(2)}) %all-to-all-start) | async-done | bytes 131104 | tf_op jit(solution)/shard_map/all_to_all | solution.py:91
  164.4 17.1 %reshape.197 = bf16[16384,1,4]{2,1,0:T(2,128)(2,1)} reshape(bf16[64,2,512]{2,1,0:T(2,128)(2,1)S(1)} %all-to-all-done) | data formatting | bytes 262144
  181.5 11.0 %slice.394 = f32[3,1,16384]{0,1,2:T(1,128)} slice(bf16[4,1,16384]{0,1,2:T(2,128)(2,1)} %bitcast.199), slice={[0:3], [0:1], [0:16384]} | slice | bytes 393216 | tf_op jit(solution)/shard_map/slice | solution.py:97
  192.6 0.0 copy-done.1
  192.6 233.5 %slice_reduce_fusion.1 = bf16[16384]{0:T(1024)(128)(2,1)S(1)} fusion(bf16[4,1,16384]{0,1,2:T(2,128)(2,1)S(1)} %bitcast.200), kind=kLoop, calls=%fused_computation.1 | loop fusion | bytes 65536 | tf_op jit(solution)/shard_map/slice | solution.py:94
  426.0 9.9 %bitcast_convert_fusion = f32[4,1,16384]{0,1,2:T(1,128)} fusion(bf16[16384,1,4]{2,1,0:T(2,128)(2,1)S(1)} %copy-done.1), kind=kLoop, calls=%fused_computation.204 | loop fusion | flops 65536 | bytes 393216 | tf_op jit(solution)/shard_map/convert_element_type | solution.py:93
  435.9 5.2 copy.100
  441.1 234.7 %slice_reduce_fusion = f32[16384]{0:T(1024)S(1)} fusion(f32[4,1,16384]{0,1,2:T(1,128)} %bitcast_convert_fusion), kind=kLoop, calls=%fused_computation | loop fusion | bytes 131072 | tf_op jit(solution)/shard_map/slice | solution.py:94
  675.9 0.2 fusion
  676.2 0.6 pad_maximum_fusion.3
  (33 shorter events, 0.5 us)
Async XLA Ops:
  0.0 8.7 %copy-start = (f32[4,16]{1,0:T(4,128)S(1)}, f32[4,16]{1,0:T(4,128)}, u32[]{:S(2)}) copy-start(f32[4,16]{1,0:T(4,128)} %param.8) | copy-start | bytes 772
  0.8 9.7 %collective-permute-start = (bf16[1,16,1024]{2,1,0:T(8,128)(2,1)S(1)}, bf16[1,16,1024]{2,1,0:T(8,128)(2,1)S(1)}, u32[]{:S(2)}, u32[]{:S(2)}) collective-permute-start(bf16[1,16,1024]{2,1,0:T(8,128)(2,1)S(1)} %get-tuple-element.32), channel_id=1, source_target_pairs={{0,4},{4,8},{8,12},{12,16},{16,20},{20,24},{24,28},{28,32},{32,36}... | collective-permute-start | bytes 98312 | tf_op jit(solution)/shard_map/ppermute | solution.py:20
  5.7 5.7 collective-permute-start.1
  11.5 5.2 collective-permute-start.2
  14.7 4.6 collective-permute-start.3
  39.7 114.4 %copy-start.2 = (s32[1,64]{1,0:T(1,128)S(1)}, s32[1,64]{1,0:T(1,128)}, u32[]{:S(2)}) copy-start(s32[1,64]{1,0:T(1,128)} %param.9) | copy-start | bytes 772
  139.8 24.7 %all-to-all-start = ((bf16[64,2,512]{2,1,0:T(2,128)(2,1)}), bf16[64,2,512]{2,1,0:T(2,128)(2,1)S(1)}, u32[]{:S(2)}, u32[]{:S(2)}) async-start(bf16[64,2,512]{2,1,0:T(2,128)(2,1)} %reshape.196), calls=%async_computation | async-start | bytes 262144 | tf_op jit(solution)/shard_map/all_to_all | solution.py:91
  181.5 11.0 %copy-start.1 = (bf16[16384,1,4]{2,1,0:T(2,128)(2,1)S(1)}, bf16[16384,1,4]{2,1,0:T(2,128)(2,1)}, u32[]{:S(2)}) copy-start(bf16[16384,1,4]{2,1,0:T(2,128)(2,1)} %reshape.197) | copy-start | bytes 393220
where the time goes:
time: 677 us
  local copies, waits for them, and re-layouts  529 us (78%)
  other arithmetic  107 us (16%)
  starting transfers between devices  25.7 us (4%)
  waiting for transfers between devices  12.8 us (2%)
    slice x3, local copies, waits for them, and re-layouts, per_device(): depths = received[3]  468 us
    unnamed x1, other arithmetic  90.8 us
    unnamed x14, local copies, waits for them, and re-layouts  27.9 us
    slice x2, local copies, waits for them, and re-layouts, per_device(): shown = jnp.sum(weight[None] * received[:3], axis=1)  16.2 us
    all_to_all x1, starting transfers between devices, per_device(): lax.all_to_all(partial_value.astype(jnp.bfloat16), 'depth', split_axis=2,...  14.3 us
  transfers between devices with their start and end apart: 5, of which 2 were waited for; matrix products, arithmetic and copies ran while one was open for 1% of the time, Pallas kernels for 0%

commit v1 on v0

--- a/solution.py
+++ b/solution.py
@@ -88,8 +88,16 @@
     flat_colour = colour.reshape(3, pixels)
     flat_depth = depth_sum.reshape(1, pixels)
     partial_value = jnp.concatenate([flat_colour, flat_depth], axis=0)[:, None, :]
-    received = lax.all_to_all(
-        partial_value.astype(jnp.bfloat16), "depth", split_axis=2, concat_axis=1, tiled=True
+    received = jnp.concatenate(
+        lax.all_to_all(
+            jnp.stack(
+                jnp.split(partial_value.astype(jnp.bfloat16), lax.axis_size("depth"), axis=2)
+            ),
+            "depth",
+            0,
+            0,
+        ),
+        axis=1,
     ).astype(partial_value.dtype)
     depths = received[3]
     prefix = jnp.dot(before, depths, precision=lax.Precision.HIGHEST)

time: 677 us -> 86.6 us (0.13)
  local copies, waits for them, and re-layouts: 529 us -> 3.39 us
  other arithmetic: 107 us -> 44.1 us
    slice x3 -> x1, local copies, waits for them, and re-layouts: 468 us -> 0.07 us  [per_device(): depths = received[3]]
    unnamed x1 -> x63, other arithmetic: 90.8 us -> 37.1 us
    unnamed x14 -> x13, local copies, waits for them, and re-layouts: 27.9 us -> 1.12 us
    slice x2 -> x0, local copies, waits for them, and re-layouts: 16.2 us -> none  [per_device(): shown = jnp.sum(weight[None] * received[:3], axis=1)]
    concatenate x1 -> x0, local copies, waits for them, and re-layouts: 13.2 us -> none  [per_device(): jnp.concatenate([flat_colour, flat_depth], axis=0)[:, None, :]]
    convert_element_type x1, other arithmetic: 9.87 us -> 0.02 us  [per_device(): received = jnp.concatenate(lax.all_to_all(jnp.stack(jnp.split(partial_val...]
  transfers between devices with their start and end apart: 5 -> 5, of which waited for: 2 -> 3; matrix products, arithmetic and copies ran while one was open for 1% -> 3% of each run, Pallas kernels for 0% -> 0%
where the time goes in v1:
time: 86.6 us; the launch traced here: 86.1 us
  other arithmetic  44.1 us (51%)
  starting transfers between devices  25.2 us (29%)
  waiting for transfers between devices  10.8 us (12%)
  local copies, waits for them, and re-layouts  3.39 us (4%)
  matrix products  1.85 us (2%)
    unnamed x63, other arithmetic  37.1 us
    all_to_all x1, starting transfers between devices, per_device(): lax.all_to_all(jnp.stack(jnp.split(partial_value.astype(jnp.bfloat16), la...  13.1 us
    all_to_all x1, waiting for transfers between devices, per_device(): lax.all_to_all(jnp.stack(jnp.split(partial_value.astype(jnp.bfloat16), la...  9.58 us
    ppermute x2, starting transfers between devices, with_halo(): lax.ppermute(tail, axis, [(i, (i + 1) % count) for i in range(ends)])  8.9 us
    ppermute x2, starting transfers between devices, with_halo(): lax.ppermute(head, axis, [((i + 1) % count, i) for i in range(ends)])  3.21 us
    add x4, other arithmetic, shear_plane(): return (1.0 - fraction) * first + fraction * second  1.88 us
  transfers between devices with their start and end apart: 5, of which 3 were waited for; matrix products, arithmetic and copies ran while one was open for 3% of the time, Pallas kernels for 0%

profile of v1, /device:TPU:1, one launch (start us, length us, event | category | flops | bytes accessed | tf_op | source)
XLA Modules:
  0.0 86.1 jit_solution(4554565502898780992)
XLA Ops:
  0.0 0.8 fusion.152
  0.8 4.9 %collective-permute-start = (bf16[1,16,1024]{2,1,0:T(8,128)(2,1)S(1)}, bf16[1,16,1024]{2,1,0:T(8,128)(2,1)S(1)}, u32[]{:S(2)}, u32[]{:S(2)}) collective-permute-start(bf16[1,16,1024]{2,1,0:T(8,128)(2,1)S(1)} %get-tuple-element.32), channel_id=1, source_target_pairs={{0,4},{4,8},{8,12},{12,16},{16,20},{20,24},{24,28},{28,32},{32,36}... | collective-permute-start | bytes 98312 | tf_op jit(solution)/shard_map/ppermute | solution.py:20
  5.7 1.9 %collective-permute-start.1 = (bf16[1,16,1024]{2,1,0:T(8,128)(2,1)S(1)}, bf16[1,16,1024]{2,1,0:T(8,128)(2,1)S(1)}, u32[]{:S(2)}, u32[]{:S(2)}) collective-permute-start(bf16[1,16,1024]{2,1,0:T(8,128)(2,1)S(1)} %get-tuple-element.31), channel_id=1, source_target_pairs={{4,0},{8,4},{12,8},{16,12},{20,16},{24,20},{28,24},{32,28},{36,32}... | collective-permute-start | bytes 98312 | tf_op jit(solution)/shard_map/ppermute | solution.py:22
  10.0 1.0 %collective-permute-done.1 = bf16[1,16,1024]{2,1,0:T(8,128)(2,1)S(1)} collective-permute-done((bf16[1,16,1024]{2,1,0:T(8,128)(2,1)S(1)}, bf16[1,16,1024]{2,1,0:T(8,128)(2,1)S(1)}, u32[]{:S(2)}, u32[]{:S(2)}) %collective-permute-start.1) | collective-permute-done | bytes 32800 | tf_op jit(solution)/shard_map/ppermute | solution.py:22
  11.0 1.3 %collective-permute-start.3 = (bf16[6,1,1024]{2,1,0:T(2,128)(2,1)S(1)}, bf16[6,1,1024]{2,1,0:T(2,128)(2,1)S(1)}, u32[]{:S(2)}, u32[]{:S(2)}) collective-permute-start(bf16[6,1,1024]{2,1,0:T(2,128)(2,1)S(1)} %get-tuple-element.30), channel_id=1, source_target_pairs={{1,0},{2,1},{3,2},{5,4},{6,5},{7,6},{9,8},{10,9},{11,10},{13,12},{... | collective-permute-start | bytes 36872 | tf_op jit(solution)/shard_map/ppermute | solution.py:22
  12.3 4.0 %collective-permute-start.2 = (bf16[6,1,1024]{2,1,0:T(2,128)(2,1)S(1)}, bf16[6,1,1024]{2,1,0:T(2,128)(2,1)S(1)}, u32[]{:S(2)}, u32[]{:S(2)}) collective-permute-start(bf16[6,1,1024]{2,1,0:T(2,128)(2,1)S(1)} %get-tuple-element.29), channel_id=1, source_target_pairs={{0,1},{1,2},{2,3},{4,5},{5,6},{6,7},{8,9},{9,10},{10,11},{12,13},{... | collective-permute-start | bytes 36872 | tf_op jit(solution)/shard_map/ppermute | solution.py:20
  18.3 0.7 fusion.21
  20.1 0.7 fusion.9
  21.2 0.7 fusion.29
  22.6 0.7 fusion.33
  23.9 0.6 constant_dynamic-update-slice_fusion.66
  24.4 0.6 constant_dynamic-update-slice_fusion.65
  25.6 0.6 constant_dynamic-update-slice_fusion.63
  26.2 0.6 constant_dynamic-update-slice_fusion.62
  26.8 0.6 constant_dynamic-update-slice_fusion.61
  27.4 0.6 constant_dynamic-update-slice_fusion.60
  29.1 0.6 constant_dynamic-update-slice_fusion.57
  30.3 0.6 constant_dynamic-update-slice_fusion.55
  30.9 0.6 constant_dynamic-update-slice_fusion.54
  31.5 0.6 constant_dynamic-update-slice_fusion.53
  32.1 0.6 constant_dynamic-update-slice_fusion.52
  32.7 0.6 constant_dynamic-update-slice_fusion.51
  33.3 0.6 constant_dynamic-update-slice_fusion.50
  33.8 0.6 constant_dynamic-update-slice_fusion.49
  34.5 0.6 constant_dynamic-update-slice_fusion.48
  35.0 0.6 constant_dynamic-update-slice_fusion.47
  35.6 0.6 constant_dynamic-update-slice_fusion.46
  36.8 0.6 constant_dynamic-update-slice_fusion.44
  37.4 0.6 constant_dynamic-update-slice_fusion.43
  38.0 0.6 constant_dynamic-update-slice_fusion.42
  38.6 0.6 constant_dynamic-update-slice_fusion.41
  39.2 0.6 constant_dynamic-update-slice_fusion.40
  39.8 0.6 constant_dynamic-update-slice_fusion.39
  40.9 0.6 constant_dynamic-update-slice_fusion.37
  42.1 0.6 constant_dynamic-update-slice_fusion.35
  42.7 0.6 constant_dynamic-update-slice_fusion.34
  43.9 0.6 constant_dynamic-update-slice_fusion.32
  45.0 0.6 constant_dynamic-update-slice_fusion.30
  45.6 0.6 constant_dynamic-update-slice_fusion.29
  46.2 0.6 constant_dynamic-update-slice_fusion.28
  46.8 0.6 constant_dynamic-update-slice_fusion.27
  47.4 0.6 constant_dynamic-update-slice_fusion.26
  48.0 0.6 constant_dynamic-update-slice_fusion.25
  48.6 0.6 constant_dynamic-update-slice_fusion.24
  49.8 0.6 constant_dynamic-update-slice_fusion.22
  50.4 0.6 constant_dynamic-update-slice_fusion.21
  51.0 0.6 constant_dynamic-update-slice_fusion.20
  51.5 0.6 constant_dynamic-update-slice_fusion.19
  52.1 0.6 constant_dynamic-update-slice_fusion.18
  52.7 0.6 constant_dynamic-update-slice_fusion.17
  53.3 0.6 constant_dynamic-update-slice_fusion.16
  53.9 0.6 constant_dynamic-update-slice_fusion.15
  55.1 0.6 constant_dynamic-update-slice_fusion.13
  56.3 0.6 constant_dynamic-update-slice_fusion.11
  57.4 0.6 constant_dynamic-update-slice_fusion.9
  58.6 0.6 constant_dynamic-update-slice_fusion.7
  59.2 0.6 constant_dynamic-update-slice_fusion.6
  59.8 0.6 constant_dynamic-update-slice_fusion.5
  60.4 0.6 constant_dynamic-update-slice_fusion.4
  61.0 0.6 constant_dynamic-update-slice_fusion.3
  61.6 13.1 %all-to-all-start = ((bf16[64,4,1,256]{3,1,2,0:T(4,128)(2,1)}), bf16[64,4,1,256]{3,1,2,0:T(4,128)(2,1)S(1)}, u32[]{:S(2)}, u32[]{:S(2)}) async-start(bf16[64,4,1,256]{3,1,2,0:T(4,128)(2,1)} %constant_dynamic-update-slice_fusion.3), calls=%async_computation | async-start | bytes 262144 | tf_op jit(solution)/shard_map/all_to_all | solution.py:92
  74.7 0.6 copy-done.3
  75.4 9.6 %all-to-all-done = bf16[64,4,1,256]{3,1,2,0:T(4,128)(2,1)S(1)} async-done(((bf16[64,4,1,256]{3,1,2,0:T(4,128)(2,1)}), bf16[64,4,1,256]{3,1,2,0:T(4,128)(2,1)S(1)}, u32[]{:S(2)}, u32[]{:S(2)}) %all-to-all-start) | async-done | bytes 131104 | tf_op jit(solution)/shard_map/all_to_all | solution.py:92
  85.5 0.6 pad_maximum_fusion.2
  (88 shorter events, 15.3 us)
Async XLA Ops:
  0.0 7.8 %copy-start = (f32[4,16]{1,0:T(4,128)S(1)}, f32[4,16]{1,0:T(4,128)}, u32[]{:S(2)}) copy-start(f32[4,16]{1,0:T(4,128)} %param.8) | copy-start | bytes 772
  0.0 7.7 %copy-start.2 = (s32[4,16,1024]{2,1,0:T(8,128)S(1)}, s32[4,16,1024]{2,1,0:T(8,128)}, u32[]{:S(2)}) copy-start(s32[4,16,1024]{2,1,0:T(8,128)} %param.7) | copy-start | bytes 786436
  0.8 8.7 %collective-permute-start = (bf16[1,16,1024]{2,1,0:T(8,128)(2,1)S(1)}, bf16[1,16,1024]{2,1,0:T(8,128)(2,1)S(1)}, u32[]{:S(2)}, u32[]{:S(2)}) collective-permute-start(bf16[1,16,1024]{2,1,0:T(8,128)(2,1)S(1)} %get-tuple-element.32), channel_id=1, source_target_pairs={{0,4},{4,8},{8,12},{12,16},{16,20},{20,24},{24,28},{28,32},{32,36}... | collective-permute-start | bytes 98312 | tf_op jit(solution)/shard_map/ppermute | solution.py:20
  5.7 5.2 %collective-permute-start.1 = (bf16[1,16,1024]{2,1,0:T(8,128)(2,1)S(1)}, bf16[1,16,1024]{2,1,0:T(8,128)(2,1)S(1)}, u32[]{:S(2)}, u32[]{:S(2)}) collective-permute-start(bf16[1,16,1024]{2,1,0:T(8,128)(2,1)S(1)} %get-tuple-element.31), channel_id=1, source_target_pairs={{4,0},{8,4},{12,8},{16,12},{20,16},{24,20},{28,24},{32,28},{36,32}... | collective-permute-start | bytes 98312 | tf_op jit(solution)/shard_map/ppermute | solution.py:22
  9.1 0.9 %copy-start.1 = (bf16[4,16,1024]{2,1,0:T(8,128)(2,1)S(1)}, bf16[4,16,1024]{2,1,0:T(8,128)(2,1)}, u32[]{:S(2)}) copy-start(bf16[4,16,1024]{2,1,0:T(8,128)(2,1)} %param.6) | copy-start | bytes 393220
  11.0 5.9 %collective-permute-start.3 = (bf16[6,1,1024]{2,1,0:T(2,128)(2,1)S(1)}, bf16[6,1,1024]{2,1,0:T(2,128)(2,1)S(1)}, u32[]{:S(2)}, u32[]{:S(2)}) collective-permute-start(bf16[6,1,1024]{2,1,0:T(2,128)(2,1)S(1)} %get-tuple-element.30), channel_id=1, source_target_pairs={{1,0},{2,1},{3,2},{5,4},{6,5},{7,6},{9,8},{10,9},{11,10},{13,12},{... | collective-permute-start | bytes 36872 | tf_op jit(solution)/shard_map/ppermute | solution.py:22
  12.3 4.9 %collective-permute-start.2 = (bf16[6,1,1024]{2,1,0:T(2,128)(2,1)S(1)}, bf16[6,1,1024]{2,1,0:T(2,128)(2,1)S(1)}, u32[]{:S(2)}, u32[]{:S(2)}) collective-permute-start(bf16[6,1,1024]{2,1,0:T(2,128)(2,1)S(1)} %get-tuple-element.29), channel_id=1, source_target_pairs={{0,1},{1,2},{2,3},{4,5},{5,6},{6,7},{8,9},{9,10},{10,11},{12,13},{... | collective-permute-start | bytes 36872 | tf_op jit(solution)/shard_map/ppermute | solution.py:20
  61.6 23.4 %all-to-all-start = ((bf16[64,4,1,256]{3,1,2,0:T(4,128)(2,1)}), bf16[64,4,1,256]{3,1,2,0:T(4,128)(2,1)S(1)}, u32[]{:S(2)}, u32[]{:S(2)}) async-start(bf16[64,4,1,256]{3,1,2,0:T(4,128)(2,1)} %constant_dynamic-update-slice_fusion.3), calls=%async_computation | async-start | bytes 262144 | tf_op jit(solution)/shard_map/all_to_all | solution.py:92
  74.7 0.7 copy-start.3
